TPU v7x, 32 devices: a whole 2x2x4 slice. The times are simulated.
32 devices in a mesh: seq: 16 (over z, y, core), tp: 2 (over x).
Axes of the slice: x: 2, y: 2, z: 4, core: 2. Of those that a mesh axis runs over, the one named last changes fastest.
Arguments:
- layer_in: bfloat16 [32768, 768], P(('seq', 'tp')), may hold values from -6 to 6
- skip_values: bfloat16 [32768, 384], P('seq', 'tp'), may hold values from -6 to 6
- block_slot: int32 [16, 8], replicated, may hold values from 0 to 3, as said below
- doc_lengths: int32 [32, 4], replicated, may hold values from 1 to 512, 1024 in all within a row
- gain_attention: float32 [768], replicated, may hold values from 0.5 to 1.5
- shift_attention: float32 [768], replicated, may hold values from -1.5 to 1.5
- query_weight: bfloat16 [768, 768], P(None, 'tp'), may hold values from -0.21875 to 0.21875
- query_bias: float32 [768], P('tp'), may hold values from -1.5 to 1.5
- key_weight: bfloat16 [768, 768], P(None, 'tp'), may hold values from -0.21875 to 0.21875
- value_weight: bfloat16 [768, 384], P(None, 'tp'), may hold values from -0.21875 to 0.21875
- value_bias: float32 [384], P('tp'), may hold values from -1.5 to 1.5
- out_weight: bfloat16 [768, 768], P('tp'), may hold values from -1.75 to 1.75
- out_bias: float32 [768], replicated, may hold values from -1.5 to 1.5
- gain_feed: float32 [768], replicated, may hold values from 0.5 to 1.5
- shift_feed: float32 [768], replicated, may hold values from -1.5 to 1.5
- up_weight: bfloat16 [768, 3072], P(None, 'tp'), may hold values from -0.21875 to 0.21875
- up_bias: float32 [3072], P('tp'), may hold values from -1.5 to 1.5
- down_weight: bfloat16 [3072, 768], P('tp'), may hold values from -0.109375 to 0.109375
- down_bias: float32 [768], replicated, may hold values from -1.5 to 1.5
- out_grad: bfloat16 [32768, 768], P(('seq', 'tp')), may hold values from -6 to 6
Outputs:
- layer_out: bfloat16 [32768, 768], P(('seq', 'tp'))
- input_grad: float32 [32768, 768], P(('seq', 'tp'))
- skip_grad: float32 [32768, 384], P('seq', 'tp')
- grad_gain_attention: float32 [768], replicated
- grad_shift_attention: float32 [768], replicated
- grad_query_weight: float32 [768, 768], P(None, 'tp')
- grad_query_bias: float32 [768], P('tp')
- grad_key_weight: float32 [768, 768], P(None, 'tp')
- grad_value_weight: float32 [768, 384], P(None, 'tp')
- grad_value_bias: float32 [384], P('tp')
- grad_out_weight: float32 [768, 768], P('tp')
- grad_out_bias: float32 [768], replicated
- grad_gain_feed: float32 [768], replicated
- grad_shift_feed: float32 [768], replicated
- grad_up_weight: float32 [768, 3072], P(None, 'tp')
- grad_up_bias: float32 [3072], P('tp')
- grad_down_weight: float32 [3072, 768], P('tp')
- grad_down_bias: float32 [768], replicated
Inputs may be any that keep to these rules, and one draw needn't show every extreme that they name: `block_slot`: for each group of 4 consecutive rows (the seq indices that hold one set of sequences) and each column, the entries are a permutation of 0 to 3. `doc_lengths`: each row gives the lengths of the documents of one sequence in order; a row sums to 1024.
All inputs are finite; a program needn't handle non-finite values.
Results may differ from a plain program's by a relative error of at most 0.015.
Values may be sent and summed in bfloat16 or wider, within the bound.
No kernel may reach another device: no remote copies, remote signals or barrier semaphores. Data moves between devices by JAX's collectives and lax.ppermute only.
A program may use at most 320 MiB of HBM per device.

v0:
```python
from functools import partial
from functools import reduce
import jax
import jax.numpy as jnp
from jax import lax
from jax.sharding import PartitionSpec as P

HEAD = 64
SEQ_LEN = 1024
BLOCK = 256
EPSILON = 1e-05


def from_partner(block, axis, apart):
    count = lax.axis_size(axis)
    route = []
    for low in range(count):
        high = low | 1 << apart
        if high != low and high < count:
            route += [(low, high), (high, low)]
    return lax.ppermute(block, axis, route)


def product(left, right):
    return jnp.dot(left, right, preferred_element_type=jnp.float32)


def product_rt(left, right):
    return lax.dot_general(
        left, right, (((1,), (1,)), ((), ())), preferred_element_type=jnp.float32
    )


def product_lt(left, right):
    return lax.dot_general(
        left, right, (((0,), (0,)), ((), ())), preferred_element_type=jnp.float32
    )


def norm_rows(rows, gain, shift):
    centred = rows - jnp.mean(rows, axis=-1, keepdims=True)
    inverse = lax.rsqrt(jnp.mean(centred * centred, axis=-1, keepdims=True) + EPSILON)
    scaled = centred * inverse
    return (scaled * gain + shift, scaled, inverse)


def norm_back(grad_out, scaled, inverse, gain):
    grad_scaled = grad_out * gain
    first_mean = jnp.mean(grad_scaled, axis=-1, keepdims=True)
    second_mean = jnp.mean(grad_scaled * scaled, axis=-1, keepdims=True)
    return inverse * (grad_scaled - first_mean - scaled * second_mean)


def block_places(slots, bounds):
    within = jnp.arange(BLOCK, dtype=jnp.int32)
    places = slots[:, None] * BLOCK + within[None, :]
    doc_ids = jnp.sum((places[:, :, None] >= bounds[:, None, :]).astype(jnp.int32), axis=2)
    return (places, doc_ids)


def swap_blocks(held, level):
    return from_partner(held, "seq", level)


def swap_grads(held, level):
    return from_partner(held.astype(jnp.bfloat16), "seq", level).astype(held.dtype)


def per_device(
    layer_in,
    skip_values,
    block_slot,
    doc_lengths,
    gain_attention,
    shift_attention,
    query_weight,
    query_bias,
    key_weight,
    value_weight,
    value_bias,
    out_weight,
    out_bias,
    gain_feed,
    shift_feed,
    up_weight,
    up_bias,
    down_weight,
    down_bias,
    out_grad,
):
    seq_span = SEQ_LEN // BLOCK
    span_levels = seq_span.bit_length() - 1
    level_order = list(range(span_levels))
    seq_batch = skip_values.shape[0] // BLOCK
    rows_all = seq_batch * BLOCK
    heads_here = query_weight.shape[1] // HEAD
    fresh_cols = value_weight.shape[1]
    score_scale = HEAD ** (-0.5)
    my_index = lax.axis_index("seq")
    my_member = my_index % seq_span
    group_id = my_index // seq_span
    lengths_here = lax.dynamic_slice_in_dim(doc_lengths, group_id * seq_batch, seq_batch, 0)
    bounds = jnp.cumsum(lengths_here, axis=1)[:, :-1]

    def places_of(member_id):
        slots = lax.dynamic_index_in_dim(
            block_slot, group_id * seq_span + member_id, 0, keepdims=False
        )
        return block_places(slots, bounds)

    own_places, own_docs = places_of(my_member)

    def visible_of(member_id):
        key_places, key_docs = places_of(member_id)
        return (key_places[:, None, :] <= own_places[:, :, None]) & (
            key_docs[:, None, :] == own_docs[:, :, None]
        )

    def heads_view(rows):
        return rows.reshape(seq_batch, BLOCK, heads_here, HEAD)

    input_float = layer_in.astype(jnp.float32)
    first_norm, first_scaled, first_inverse = norm_rows(
        input_float, gain_attention, shift_attention
    )
    first_rows = lax.all_gather(first_norm.astype(jnp.bfloat16), "tp", axis=0, tiled=True)
    queries = (product(first_rows, query_weight) + query_bias).astype(jnp.bfloat16)
    keys_here = product(first_rows, key_weight).astype(jnp.bfloat16)
    fresh = (product(first_rows, value_weight) + value_bias).astype(jnp.bfloat16)
    values_here = jnp.concatenate([fresh, skip_values], axis=1)
    query_heads = heads_view(queries)
    sources = [(heads_view(keys_here), heads_view(values_here), visible_of(my_member))]
    held = jnp.stack([keys_here, values_here])[None]
    for level in level_order:
        held = jnp.concatenate([held, swap_blocks(held, level)], axis=0)
    for slot in range(1, seq_span):
        partner = 0
        for step in range(span_levels):
            partner = partner + ((slot >> step & 1) << level_order[step])
        sources.append(
            (
                heads_view(held[slot, 0]),
                heads_view(held[slot, 1]),
                visible_of(jnp.bitwise_xor(my_member, partner)),
            )
        )

    def scores_of(key_heads, seen_mask):
        raw = (
            jnp.einsum(
                "bqhe,bkhe->bhqk", query_heads, key_heads, preferred_element_type=jnp.float32
            )
            * score_scale
        )
        return jnp.where(seen_mask[:, None], raw, -jnp.inf)

    score_list = [scores_of(key_heads, seen_mask) for key_heads, value_heads, seen_mask in sources]
    row_max = reduce(jnp.maximum, [jnp.max(scores, axis=-1) for scores in score_list])
    row_total = reduce(
        jnp.add, [jnp.sum(jnp.exp(scores - row_max[..., None]), axis=-1) for scores in score_list]
    )
    log_total = row_max + jnp.log(row_total)
    attended = reduce(
        jnp.add,
        [
            jnp.einsum(
                "bhqk,bkhe->bqhe",
                jnp.exp(scores - log_total[..., None]).astype(jnp.bfloat16),
                source[1],
                preferred_element_type=jnp.float32,
            )
            for scores, source in zip(score_list, sources)
        ],
    )
    attended_rows = attended.reshape(rows_all, heads_here * HEAD).astype(jnp.bfloat16)
    middle = (
        input_float
        + lax.psum_scatter(
            product(attended_rows, out_weight).astype(jnp.bfloat16),
            "tp",
            scatter_dimension=0,
            tiled=True,
        ).astype(jnp.float32)
        + out_bias
    )
    second_norm, second_scaled, second_inverse = norm_rows(middle, gain_feed, shift_feed)
    second_rows = lax.all_gather(second_norm.astype(jnp.bfloat16), "tp", axis=0, tiled=True)
    hidden = product(second_rows, up_weight) + up_bias
    activated, gelu_back = jax.vjp(partial(jax.nn.gelu, approximate=True), hidden)
    activated_low = activated.astype(jnp.bfloat16)
    feed_out = lax.psum_scatter(
        product(activated_low, down_weight).astype(jnp.bfloat16),
        "tp",
        scatter_dimension=0,
        tiled=True,
    ).astype(jnp.float32)
    layer_out = (middle + feed_out + down_bias).astype(jnp.bfloat16)
    grad_output = out_grad.astype(jnp.float32)
    grad_down_bias = jnp.sum(grad_output, axis=0)
    grad_rows_all = lax.all_gather(out_grad, "tp", axis=0, tiled=True)
    grad_down_weight = product_lt(activated_low, grad_rows_all)
    grad_hidden = gelu_back(product_rt(grad_rows_all, down_weight))[0]
    grad_up_bias = jnp.sum(grad_hidden, axis=0)
    hidden_low = grad_hidden.astype(jnp.bfloat16)
    grad_up_weight = product_lt(second_rows, hidden_low)
    second_grad = lax.psum_scatter(
        product_rt(hidden_low, up_weight).astype(jnp.bfloat16),
        "tp",
        scatter_dimension=0,
        tiled=True,
    ).astype(jnp.float32)
    grad_gain_feed = jnp.sum(second_grad * second_scaled, axis=0)
    grad_shift_feed = jnp.sum(second_grad, axis=0)
    middle_grad = grad_output + norm_back(second_grad, second_scaled, second_inverse, gain_feed)
    grad_out_bias = jnp.sum(middle_grad, axis=0)
    middle_rows = lax.all_gather(middle_grad.astype(jnp.bfloat16), "tp", axis=0, tiled=True)
    grad_out_weight = product_lt(attended_rows, middle_rows)
    grad_heads = heads_view(product_rt(middle_rows, out_weight).astype(jnp.bfloat16))
    prob_list = []
    dprob_list = []
    for key_heads, value_heads, seen_mask in sources:
        prob_list.append(jnp.exp(scores_of(key_heads, seen_mask) - log_total[..., None]))
        dprob_list.append(
            jnp.einsum(
                "bqhe,bkhe->bhqk", grad_heads, value_heads, preferred_element_type=jnp.float32
            )
        )
    delta = reduce(
        jnp.add, [jnp.sum(probs * dprobs, axis=-1) for probs, dprobs in zip(prob_list, dprob_list)]
    )
    query_parts = []
    pair_grads = []
    for probs, dprobs, source in zip(prob_list, dprob_list, sources):
        dscores = (probs * (dprobs - delta[..., None])).astype(jnp.bfloat16)
        query_parts.append(
            jnp.einsum("bhqk,bkhe->bqhe", dscores, source[0], preferred_element_type=jnp.float32)
            * score_scale
        )
        key_part = (
            jnp.einsum("bhqk,bqhe->bkhe", dscores, query_heads, preferred_element_type=jnp.float32)
            * score_scale
        )
        value_part = jnp.einsum(
            "bhqk,bqhe->bkhe",
            probs.astype(jnp.bfloat16),
            grad_heads,
            preferred_element_type=jnp.float32,
        )
        pair_grads.append(jnp.stack([key_part, value_part]))
    held_grads = jnp.stack(pair_grads)
    for step in reversed(range(span_levels)):
        half = 1 << step
        held_grads = held_grads[:half] + swap_grads(held_grads[half:], level_order[step])
    pair_total = held_grads[0]
    query_grad = reduce(jnp.add, query_parts).reshape(rows_all, heads_here * HEAD)
    key_grad = pair_total[0].reshape(rows_all, heads_here * HEAD)
    value_grad = pair_total[1].reshape(rows_all, heads_here * HEAD)
    fresh_grad = value_grad[:, :fresh_cols]
    skip_grad = value_grad[:, fresh_cols:]
    grad_query_bias = jnp.sum(query_grad, axis=0)
    grad_value_bias = jnp.sum(fresh_grad, axis=0)
    query_low = query_grad.astype(jnp.bfloat16)
    key_low = key_grad.astype(jnp.bfloat16)
    fresh_low = fresh_grad.astype(jnp.bfloat16)
    grad_query_weight = product_lt(first_rows, query_low)
    grad_key_weight = product_lt(first_rows, key_low)
    grad_value_weight = product_lt(first_rows, fresh_low)
    first_terms = (
        product_rt(query_low, query_weight)
        + product_rt(key_low, key_weight)
        + product_rt(fresh_low, value_weight)
    )
    first_grad = lax.psum_scatter(
        first_terms.astype(jnp.bfloat16), "tp", scatter_dimension=0, tiled=True
    ).astype(jnp.float32)
    grad_gain_attention = jnp.sum(first_grad * first_scaled, axis=0)
    grad_shift_attention = jnp.sum(first_grad, axis=0)
    input_grad = middle_grad + norm_back(first_grad, first_scaled, first_inverse, gain_attention)
    (
        grad_query_weight,
        grad_query_bias,
        grad_key_weight,
        grad_value_weight,
        grad_value_bias,
        grad_out_weight,
        grad_up_weight,
        grad_up_bias,
        grad_down_weight,
    ) = lax.psum(
        (
            grad_query_weight,
            grad_query_bias,
            grad_key_weight,
            grad_value_weight,
            grad_value_bias,
            grad_out_weight,
            grad_up_weight,
            grad_up_bias,
            grad_down_weight,
        ),
        "seq",
    )
    (
        grad_gain_attention,
        grad_shift_attention,
        grad_gain_feed,
        grad_shift_feed,
        grad_out_bias,
        grad_down_bias,
    ) = lax.psum(
        (
            grad_gain_attention,
            grad_shift_attention,
            grad_gain_feed,
            grad_shift_feed,
            grad_out_bias,
            grad_down_bias,
        ),
        ("seq", "tp"),
    )
    return (
        layer_out,
        input_grad,
        skip_grad,
        grad_gain_attention,
        grad_shift_attention,
        grad_query_weight,
        grad_query_bias,
        grad_key_weight,
        grad_value_weight,
        grad_value_bias,
        grad_out_weight,
        grad_out_bias,
        grad_gain_feed,
        grad_shift_feed,
        grad_up_weight,
        grad_up_bias,
        grad_down_weight,
        grad_down_bias,
    )


def solution(mesh):
    return jax.shard_map(
        per_device,
        mesh=mesh,
        in_specs=(
            P(("seq", "tp"), None),
            P("seq", "tp"),
            P(),
            P(),
            P(),
            P(),
            P(None, "tp"),
            P("tp"),
            P(None, "tp"),
            P(None, "tp"),
            P("tp"),
            P("tp", None),
            P(),
            P(),
            P(),
            P(None, "tp"),
            P("tp"),
            P("tp", None),
            P(),
            P(("seq", "tp"), None),
        ),
        out_specs=(
            P(("seq", "tp"), None),
            P(("seq", "tp"), None),
            P("seq", "tp"),
            P(),
            P(),
            P(None, "tp"),
            P("tp"),
            P(None, "tp"),
            P(None, "tp"),
            P("tp"),
            P("tp", None),
            P(),
            P(),
            P(),
            P(None, "tp"),
            P("tp"),
            P("tp", None),
            P(),
        ),
        check_vma=False,
    )
```

profile of v0, /device:TPU:0, one launch (start us, length us, event | category | flops | bytes accessed | tf_op | source)
XLA Modules:
  0.0 1259.1 jit_solution(5588381925399778991)
XLA Ops:
  13.7 47.7 %all-gather.5.cloned.1.call-done = bf16[2048,768]{1,0:T(8,128)(2,1)} async-done(((bf16[1024,768]{1,0:T(8,128)(2,1)}), bf16[2048,768]{1,0:T(8,128)(2,1)}) %all-gather.5.cloned.1.call-update) | async-done | bytes 3145744 | tf_op jit(solution)/shard_map/all_gather | solution.py:126
  69.7 5.7 collective-permute-done
  81.2 4.5 compare_and_fusion.2
  96.6 6.0 fusion.6
  103.8 6.0 fusion.7
  109.8 107.2 %collective-permute-done.1 = bf16[2,2,2048,384]{2,3,1,0:T(8,128)(2,1)} collective-permute-done((bf16[2,2,2048,384]{2,3,1,0:T(8,128)(2,1)}, bf16[2,2,2048,384]{2,3,1,0:T(8,128)(2,1)}, u32[]{:S(2)}, u32[]{:S(2)}) %collective-permute-start.1) | collective-permute-done | bytes 6291488 | tf_op jit(solution)/shard_map/ppermute | solution.py:21
  224.0 6.5 fusion.8
  233.4 20.6 %exponential_reduce_fusion.2 = (f32[8,6,256]{2,1,0:T(8,128)S(1)}, f32[8,6,256]{2,1,0:T(8,128)S(1)}, f32[8,6,256]{2,1,0:T(8,128)S(1)}, f32[8,6,256]{2,1,0:T(8,128)S(1)}) fusion(f32[8,6,256,256]{2,3,1,0:T(8,128)} %get-tuple-element.86, f32[8,6,256]{2,1,0:T(8,128)S(1)} %maximum_maximum_fusion, pred[8,256,256]{1,2,0:T(8,128)(4,1)S(1)} %copy-done.24, ...), kind=kLoop, calls=%fused_computation.24 | loop fusion | flops 50282496 | bytes 52674560 | tf_op jit(solution)/shard_map/reduce_sum | solution.py:160
  254.1 9.3 fusion.51
  263.3 9.3 fusion.55
  272.6 9.2 fusion.59
  281.9 7.9 fusion.45
  297.5 43.4 %reduce-scatter.5.cloned.1.call-done = bf16[1024,768]{1,0:T(8,128)(2,1)} async-done(((bf16[2048,768]{1,0:T(8,128)(2,1)}), bf16[1024,768]{1,0:T(8,128)(2,1)}) %reduce-scatter.5.cloned.1.call-update) | async-done | bytes 1572880 | tf_op jit(solution)/shard_map/reduce_scatter | solution.py:178
  347.3 44.5 %all-gather.7.cloned.1.call-done = bf16[2048,768]{1,0:T(8,128)(2,1)} async-done(((bf16[1024,768]{1,0:T(8,128)(2,1)}), bf16[2048,768]{1,0:T(8,128)(2,1)}) %all-gather.7.cloned.1.call-update) | async-done | bytes 3145744 | tf_op jit(solution)/shard_map/all_gather | solution.py:187
  391.8 13.3 %multiply_convert_fusion.4 = (bf16[2048,1536]{1,0:T(8,128)(2,1)}, f32[2048,1536]{1,0:T(8,128)}) fusion(f32[1536]{0:T(1024)S(1)} %copy-done.80, bf16[2048,768]{1,0:T(8,128)(2,1)} %all-gather.7.cloned.1.call-done, bf16[768,1536]{1,0:T(8,128)(2,1)S(1)} %copy-done), kind=kOutput, calls=%fused_computation.17 | convolution fusion | flops 4863295488 | bytes 24385536 | tf_op jit(solution)/shard_map/dot_general | solution.py:25
  405.1 33.1 %all-gather.9.cloned.1.call-done = bf16[2048,768]{1,0:T(8,128)(2,1)} async-done(((bf16[1024,768]{1,0:T(8,128)(2,1)}), bf16[2048,768]{1,0:T(8,128)(2,1)}) %all-gather.9.cloned.1.call-update) | async-done | bytes 3145744 | tf_op jit(solution)/shard_map/all_gather | solution.py:200
  438.2 17.5 %fusion.107 = (f32[1536]{0:T(1024)}, bf16[2048,1536]{1,0:T(8,128)(2,1)S(1)}) fusion(f32[2048,1536]{1,0:T(8,128)} %get-tuple-element.88, f32[1536]{0:T(1024)S(1)} %copy-done.80, bf16[2048,768]{1,0:T(8,128)(2,1)} %all-gather.9.cloned.1.call-done, bf16[1536,768]{1,0:T(8,128)(2,1)} %param.37), kind=kOutput, calls=%fused_computation.199 | convolution fusion | flops 4901042688 | bytes 24391680 | tf_op jit(solution)/shard_map/dot_general | solution.py:29
  458.3 6.4 convolution_convert_fusion.1
  466.4 9.6 convolution_convert_fusion.2
  476.1 32.2 %reduce-scatter.9.cloned.1.call-done = bf16[1024,768]{1,0:T(8,128)(2,1)} async-done(((bf16[2048,768]{1,0:T(8,128)(2,1)}), bf16[1024,768]{1,0:T(8,128)(2,1)}) %reduce-scatter.9.cloned.1.call-update) | async-done | bytes 1572880 | tf_op jit(solution)/shard_map/reduce_scatter | solution.py:206
  512.3 42.0 %reduce-scatter.7.cloned.1.call-done = bf16[1024,768]{1,0:T(8,128)(2,1)} async-done(((bf16[2048,768]{1,0:T(8,128)(2,1)}), bf16[1024,768]{1,0:T(8,128)(2,1)}) %reduce-scatter.7.cloned.1.call-update) | async-done | bytes 1572880 | tf_op jit(solution)/shard_map/reduce_scatter | solution.py:191
  554.3 5.6 fusion.104
  563.0 45.0 %all-gather.11.cloned.1.call-done = bf16[2048,768]{1,0:T(8,128)(2,1)} async-done(((bf16[1024,768]{1,0:T(8,128)(2,1)}), bf16[2048,768]{1,0:T(8,128)(2,1)}) %all-gather.11.cloned.1.call-update) | async-done | bytes 3145744 | tf_op jit(solution)/shard_map/all_gather | solution.py:216
  615.3 8.9 fusion.41
  624.2 9.0 fusion.42
  633.2 6.4 fusion.49
  639.6 6.4 fusion.46
  646.0 6.6 fusion.57
  652.6 36.6 %multiply_reduce_fusion.2 = (f32[8,6,256]{2,1,0:T(8,128)S(1)}, f32[8,6,256]{2,1,0:T(8,128)S(1)}, f32[8,6,256]{2,1,0:T(8,128)S(1)}, f32[8,6,256]{2,1,0:T(8,128)S(1)}, f32[8,6,256,256]{2,3,1,0:T(8,128)}) fusion(f32[8,6,256,256]{2,3,1,0:T(8,128)} %get-tuple-element.86, f32[8,6,256]{2,1,0:T(8,128)S(1)} %log_add_fusion, pred[8,256,256]{1,2,0:T(8,128)(4,1)S(1)} %copy-done.25, ...), kind=kOutput, calls=%fused_computation.15 | convolution fusion | flops 465518592 | bytes 106151936 | tf_op jit(solution)/shard_map/bqhe,bkhe->bhqk/dot_general | solution.py:224
  689.2 42.7 %multiply_convert_fusion.1 = (bf16[8,6,256,256]{2,3,1,0:T(8,128)(2,1)}, bf16[8,6,256,256]{2,3,1,0:T(8,128)(2,1)}, bf16[8,6,256,256]{2,3,1,0:T(8,128)(2,1)}, bf16[8,6,256,256]{2,3,1,0:T(8,128)(2,1)}) fusion(f32[8,6,256,256]{2,3,1,0:T(8,128)} %fusion.49, f32[8,6,256,256]{2,3,1,0:T(8,128)} %get-tuple-element.82, f32[8,6,256]{2,1,0:T(8,128)S(1)} %add_add_fusion, ...), kind=kLoop, calls=%fused_computation.10 | loop fusion | flops 75497472 | bytes 128024576 | tf_op jit(solution)/shard_map/convert_element_type | solution.py:234
  731.9 5.0 fusion.43
  742.8 6.5 pad_maximum_fusion.1
  750.8 6.6 multiply_bitcast_fusion
  757.4 4.5 convolution_bitcast_fusion
  761.9 6.5 maximum_bitcast_fusion.1
  768.4 6.6 multiply_bitcast_fusion.1
  775.1 4.5 convolution_bitcast_fusion.1
  782.4 104.5 %collective-permute-done.2 = bf16[2,2,8,256,6,64]{3,5,4,2,1,0:T(8,128)(2,1)} collective-permute-done((bf16[2,2,8,256,6,64]{3,5,4,2,1,0:T(8,128)(2,1)}, bf16[2,2,8,256,6,64]{3,5,4,2,1,0:T(8,128)(2,1)}, u32[]{:S(2)}, u32[]{:S(2)}) %collective-permute-start.2) | collective-permute-done | bytes 6291488 | tf_op jit(solution)/shard_map/ppermute | solution.py:21
  886.9 11.3 maximum_add_fusion
  898.2 5.1 slice.79
  909.1 6.0 bitcast_convert_fusion
  918.4 5.7 slice_add_fusion
  938.2 10.0 fusion.37
  948.2 8.9 fusion.112
  972.5 64.0 %all-reduce.1 = (f32[384]{0:T(512)}, f32[192]{0:T(256)}, f32[1536]{0:T(1024)}) all-reduce(f32[384]{0:T(512)S(1)} %reduce_sum.290, f32[192]{0:T(256)S(1)} %get-tuple-element.64, f32[1536]{0:T(1024)S(1)} %copy-done.70), channel_id=1, replica_groups=mesh['seq'=16,'tp'=2] {'seq'}, use_global_device_ids=true, to_apply=%region_35.36 | all-reduce | flops 2112 | bytes 16896 | tf_op jit(solution)/shard_map/psum | solution.py:289
  1039.5 39.5 %all-reduce = (f32[768]{0:T(1024)}, f32[768]{0:T(1024)}, f32[768]{0:T(1024)}, f32[768]{0:T(1024)}, f32[768]{0:T(1024)}, /*index=5*/f32[768]{0:T(1024)}) all-reduce(f32[768]{0:T(1024)S(1)} %get-tuple-element.20, f32[768]{0:T(1024)S(1)} %get-tuple-element.25, f32[768]{0:T(1024)S(1)} %copy-done.68, ...), channel_id=1, replica_groups=mesh['seq'=16,'tp'=2] {'seq','tp'}, use_global_device_ids=true, to_apply=%region_30.31 | all-reduce | flops 4608 | bytes 36864 | tf_op jit(solution)/shard_map/psum | solution.py:310
  1079.0 4.1 fusion.28
  1083.1 158.4 %all-reduce.5.cloned.1.call-done = (f32[768,384]{1,0:T(8,128)}, f32[768,384]{1,0:T(8,128)}, f32[768,192]{0,1:T(8,128)}, f32[384,768]{1,0:T(8,128)}, f32[768,1536]{1,0:T(8,128)}, /*index=5*/f32[1536,768]{1,0:T(8,128)}) async-done(((f32[768,384]{1,0:T(8,128)}, f32[768,384]{1,0:T(8,128)}, f32[768,192]{0,1:T(8,128)}, f32[384,768]{1,0:T(8,128)}, f32[768,1536]{1,0:T(8,128)}, /*index=5*/f32[1536,768]{1,0:T(8,128)}), ...) | async-done | bytes 13565968 | tf_op jit(solution)/shard_map/psum | solution.py:289
  (321 shorter events, 137.1 us)
Async XLA Ops:
  7.2 384.6 %copy-start = (bf16[768,1536]{1,0:T(8,128)(2,1)S(1)}, bf16[768,1536]{1,0:T(8,128)(2,1)}, u32[]{:S(2)}) copy-start(bf16[768,1536]{1,0:T(8,128)(2,1)} %param.35) | copy-start | bytes 7077892
  7.2 54.2 %all-gather.5.cloned.1.call-start = ((), (), s32[]{:S(2)}) async-start(), calls=%async_computation.4 | async-start | bytes 4718592 | tf_op jit(solution)/shard_map/all_gather | solution.py:126
  9.1 52.3 %copy-start.55 = (bf16[768,192]{0,1:T(8,128)(2,1)S(1)}, bf16[768,192]{0,1:T(8,128)(2,1)}, u32[]{:S(2)}) copy-start(bf16[768,192]{0,1:T(8,128)(2,1)} %param.29) | copy-start | bytes 884740
  9.2 52.3 %copy-start.82 = (f32[192]{0:T(256)S(1)}, f32[192]{0:T(256)}, u32[]{:S(2)}) copy-start(f32[192]{0:T(256)} %param.30) | copy-start | bytes 2308
  13.7 50.9 %copy-start.50 = (bf16[2048,192]{0,1:T(8,128)(2,1)S(1)}, bf16[2048,192]{0,1:T(8,128)(2,1)}, u32[]{:S(2)}) copy-start(bf16[2048,192]{0,1:T(8,128)(2,1)} %param.21) | copy-start | bytes 2359300
  13.7 327.2 %reduce-scatter.5.cloned.1.call-start = ((), (), s32[]{:S(2)}) async-start(), calls=%async_computation.5 | async-start | bytes 4718592 | tf_op jit(solution)/shard_map/reduce_scatter | solution.py:178
  69.7 11.0 copy-start.62
  69.7 5.7 collective-permute-start
  79.1 137.9 %collective-permute-start.1 = (bf16[2,2,2048,384]{2,3,1,0:T(8,128)(2,1)}, bf16[2,2,2048,384]{2,3,1,0:T(8,128)(2,1)}, u32[]{:S(2)}, u32[]{:S(2)}) collective-permute-start(bf16[2,2,2048,384]{2,3,1,0:T(8,128)(2,1)} %pad_maximum_fusion), channel_id=1, source_target_pairs={{0,4},{4,0},{2,6},{6,2},{8,12},{12,8},{10,14},{14,10},{16,20},{20,... | collective-permute-start | bytes 18874376 | tf_op jit(solution)/shard_map/ppermute | solution.py:21
  96.0 134.4 %copy-start.8 = (bf16[48,8,8,256]{3,2,1,0:T(8,128)(2,1)}, bf16[48,8,8,256]{3,2,1,0:T(8,128)(2,1)S(1)}, u32[]{:S(2)}) copy-start(bf16[48,8,8,256]{3,2,1,0:T(8,128)(2,1)S(1)} %copy.217) | copy-start | bytes 4718596
  96.5 176.1 %copy-start.20 = (bf16[48,8,8,256]{3,2,1,0:T(8,128)(2,1)}, bf16[48,8,8,256]{3,2,1,0:T(8,128)(2,1)S(1)}, u32[]{:S(2)}) copy-start(bf16[48,8,8,256]{3,2,1,0:T(8,128)(2,1)S(1)} %copy.216) | copy-start | bytes 4718596
  103.3 160.1 %copy-start.28 = (bf16[48,8,8,256]{3,2,1,0:T(8,128)(2,1)}, bf16[48,8,8,256]{3,2,1,0:T(8,128)(2,1)S(1)}, u32[]{:S(2)}) copy-start(bf16[48,8,8,256]{3,2,1,0:T(8,128)(2,1)S(1)} %copy.222) | copy-start | bytes 4718596
  222.6 31.5 %copy-start.22 = (bf16[48,8,8,256]{3,2,1,0:T(8,128)(2,1)}, bf16[48,8,8,256]{3,2,1,0:T(8,128)(2,1)S(1)}, u32[]{:S(2)}) copy-start(bf16[48,8,8,256]{3,2,1,0:T(8,128)(2,1)S(1)} %copy.223) | copy-start | bytes 4718596
  233.4 48.5 %copy-start.2 = (f32[8,6,256,256]{2,3,1,0:T(8,128)}, f32[8,6,256,256]{2,3,1,0:T(8,128)S(1)}, u32[]{:S(2)}) copy-start(f32[8,6,256,256]{2,3,1,0:T(8,128)S(1)} %get-tuple-element.80) | copy-start | bytes 37748740
  297.4 43.5 %copy-start.59 = (f32[768]{0:T(1024)S(1)}, f32[768]{0:T(1024)}, u32[]{:S(2)}) copy-start(f32[768]{0:T(1024)} %param.32) | copy-start | bytes 9220
  297.4 47.2 %copy-start.65 = (f32[768]{0:T(1024)S(1)}, f32[768]{0:T(1024)}, u32[]{:S(2)}) copy-start(f32[768]{0:T(1024)} %param.33) | copy-start | bytes 9220
  297.4 47.2 %copy-start.73 = (f32[768]{0:T(1024)S(1)}, f32[768]{0:T(1024)}, u32[]{:S(2)}) copy-start(f32[768]{0:T(1024)} %param.34) | copy-start | bytes 9220
  297.4 94.4 %all-gather.7.cloned.1.call-start = ((), (), s32[]{:S(2)}) async-start(), calls=%async_computation.6 | async-start | bytes 4718592 | tf_op jit(solution)/shard_map/all_gather | solution.py:187
  344.6 47.2 %copy-start.80 = (f32[1536]{0:T(1024)S(1)}, f32[1536]{0:T(1024)}, u32[]{:S(2)}) copy-start(f32[1536]{0:T(1024)} %param.36) | copy-start | bytes 18436
  346.7 91.5 %all-gather.9.cloned.1.call-start = ((), (), s32[]{:S(2)}) async-start(), calls=%async_computation.8 | async-start | bytes 4718592 | tf_op jit(solution)/shard_map/all_gather | solution.py:200
  347.3 161.0 %reduce-scatter.9.cloned.1.call-start = ((), (), s32[]{:S(2)}) async-start(), calls=%async_computation.9 | async-start | bytes 4718592 | tf_op jit(solution)/shard_map/reduce_scatter | solution.py:206
  464.8 89.6 %reduce-scatter.7.cloned.1.call-start = ((), (), s32[]{:S(2)}) async-start(), calls=%async_computation.7 | async-start | bytes 4718592 | tf_op jit(solution)/shard_map/reduce_scatter | solution.py:191
  476.0 32.3 %copy-start.5 = (bf16[1024,768]{1,0:T(8,128)(2,1)S(1)}, bf16[1024,768]{1,0:T(8,128)(2,1)}, u32[]{:S(2)}) copy-start(bf16[1024,768]{1,0:T(8,128)(2,1)} %param.20) | copy-start | bytes 4718596
  476.0 78.3 %copy-start.72 = (f32[768]{0:T(1024)S(1)}, f32[768]{0:T(1024)}, u32[]{:S(2)}) copy-start(f32[768]{0:T(1024)} %param.38) | copy-start | bytes 9220
  476.0 132.0 %all-gather.11.cloned.1.call-start = ((), (), s32[]{:S(2)}) async-start(), calls=%async_computation.10 | async-start | bytes 4718592 | tf_op jit(solution)/shard_map/all_gather | solution.py:216
  561.6 46.4 %copy-start.79 = (bf16[384,768]{1,0:T(8,128)(2,1)S(1)}, bf16[384,768]{1,0:T(8,128)(2,1)}, u32[]{:S(2)}) copy-start(bf16[384,768]{1,0:T(8,128)(2,1)} %param.31) | copy-start | bytes 1769476
  562.9 473.6 %reduce-scatter.11.cloned.1.call-start = ((), (), s32[]{:S(2)}) async-start(), calls=%async_computation.11 | async-start | bytes 4718592 | tf_op jit(solution)/shard_map/reduce_scatter | solution.py:273
  689.2 42.7 %copy-start.9 = (bf16[48,8,8,256]{3,2,1,0:T(8,128)(2,1)S(1)}, bf16[48,8,8,256]{3,2,1,0:T(8,128)(2,1)}, u32[]{:S(2)}) copy-start(bf16[48,8,8,256]{3,2,1,0:T(8,128)(2,1)} %copy-done.8) | copy-start | bytes 4718596
  742.8 14.6 %slice-start.3 = ((s8[12582912]{0:T(1024)(128)(4,1)}), s8[4194304]{0:T(1024)(128)(4,1)S(1)}, s32[]{:S(2)}) async-start(s8[12582912]{0:T(1024)(128)(4,1)} %bitcast.177), calls=%async_computation.16 | async-start | bytes 8388608
  742.8 14.6 %slice-start.4 = ((s8[12582912]{0:T(1024)(128)(4,1)}), s8[4194304]{0:T(1024)(128)(4,1)S(1)}, s32[]{:S(2)}) async-start(s8[12582912]{0:T(1024)(128)(4,1)} %bitcast.177), calls=%async_computation.17 | async-start | bytes 8388608
  749.3 137.6 %collective-permute-start.2 = (bf16[2,2,8,256,6,64]{3,5,4,2,1,0:T(8,128)(2,1)}, bf16[2,2,8,256,6,64]{3,5,4,2,1,0:T(8,128)(2,1)}, u32[]{:S(2)}, u32[]{:S(2)}) collective-permute-start(bf16[2,2,8,256,6,64]{3,5,4,2,1,0:T(8,128)(2,1)} %pad_maximum_fusion.1), channel_id=1, source_target_pairs={{0,4},{4,0},{2,6},{6,2},{8,12},{12,8},{10,14},{14,10},{16,20},{20,... | collective-permute-start | bytes 18874376 | tf_op jit(solution)/shard_map/ppermute | solution.py:21
  761.9 13.1 %slice-start = ((s8[12582912]{0:T(1024)(128)(4,1)}), s8[4194304]{0:T(1024)(128)(4,1)S(1)}, s32[]{:S(2)}) async-start(s8[12582912]{0:T(1024)(128)(4,1)} %bitcast.175), calls=%async_computation.13 | async-start | bytes 8388608
  761.9 13.1 %slice-start.1 = ((s8[12582912]{0:T(1024)(128)(4,1)}), s8[4194304]{0:T(1024)(128)(4,1)S(1)}, s32[]{:S(2)}) async-start(s8[12582912]{0:T(1024)(128)(4,1)} %bitcast.175), calls=%async_computation.14 | async-start | bytes 8388608
  779.5 123.8 %slice-start.8 = ((s8[6291456]{0:T(1024)(128)(4,1)}), s8[4194304]{0:T(1024)(128)(4,1)S(1)}, s32[]{:S(2)}) async-start(s8[6291456]{0:T(1024)(128)(4,1)} %bitcast.189), calls=%async_computation.21 | async-start | bytes 8388608
  779.5 124.9 %slice-start.12 = ((s8[6291456]{0:T(1024)(128)(4,1)}), s8[4194304]{0:T(1024)(128)(4,1)S(1)}, s32[]{:S(2)}) async-start(s8[6291456]{0:T(1024)(128)(4,1)} %bitcast.193), calls=%async_computation.25 | async-start | bytes 8388608
  782.4 120.9 %slice-start.9 = ((s8[6291456]{0:T(1024)(128)(4,1)}), s8[2097152]{0:T(1024)(128)(4,1)S(1)}, s32[]{:S(2)}) async-start(s8[6291456]{0:T(1024)(128)(4,1)} %bitcast.189), calls=%async_computation.22 | async-start | bytes 4194304
  782.4 122.0 %slice-start.13 = ((s8[6291456]{0:T(1024)(128)(4,1)}), s8[2097152]{0:T(1024)(128)(4,1)S(1)}, s32[]{:S(2)}) async-start(s8[6291456]{0:T(1024)(128)(4,1)} %bitcast.193), calls=%async_computation.26 | async-start | bytes 4194304
  903.3 15.1 %collective-permute-start.3 = (bf16[1,2,8,256,6,64]{3,5,4,2,1,0:T(8,128)(2,1)}, bf16[1,2,8,256,6,64]{3,5,4,2,1,0:T(8,128)(2,1)}, u32[]{:S(2)}, u32[]{:S(2)}) collective-permute-start(bf16[1,2,8,256,6,64]{3,5,4,2,1,0:T(8,128)(2,1)} %slice.79), channel_id=1, source_target_pairs={{0,2},{2,0},{4,6},{6,4},{8,10},{10,8},{12,14},{14,12},{16,18},{18,... | collective-permute-start | bytes 9437192 | tf_op jit(solution)/shard_map/ppermute | solution.py:21
  906.3 12.1 slice-start.14
  938.1 303.4 %all-reduce.5.cloned.1.call-start = ((), (), s32[]{:S(2)}) async-start(), calls=%async_computation.12 | async-start | bytes 27131904 | tf_op jit(solution)/shard_map/psum | solution.py:289
  969.0 67.5 %copy-start.6 = (bf16[1024,768]{1,0:T(8,128)(2,1)S(1)}, bf16[1024,768]{1,0:T(8,128)(2,1)}, u32[]{:S(2)}) copy-start(bf16[1024,768]{1,0:T(8,128)(2,1)} %param.20) | copy-start | bytes 4718596
  969.0 67.5 %copy-start.58 = (f32[1024]{0:T(1024)S(1)}, f32[1024]{0:T(1024)}, u32[]{:S(2)}) copy-start(f32[1024]{0:T(1024)} %copy-done.57) | copy-start | bytes 12292
  969.0 67.5 %copy-start.61 = (f32[1024]{0:T(1024)S(1)}, f32[1024]{0:T(1024)}, u32[]{:S(2)}) copy-start(f32[1024]{0:T(1024)} %copy-done.60) | copy-start | bytes 12292
  969.0 67.5 %copy-start.64 = (f32[768]{0:T(1024)S(1)}, f32[768]{0:T(1024)}, u32[]{:S(2)}) copy-start(f32[768]{0:T(1024)} %param.24) | copy-start | bytes 9220
  969.1 70.3 %copy-start.66 = (f32[768]{0:T(1024)S(1)}, f32[768]{0:T(1024)}, u32[]{:S(2)}) copy-start(f32[768]{0:T(1024)} %get-tuple-element.18) | copy-start | bytes 9220
  969.1 70.3 %copy-start.67 = (f32[768]{0:T(1024)S(1)}, f32[768]{0:T(1024)}, u32[]{:S(2)}) copy-start(f32[768]{0:T(1024)} %get-tuple-element.24) | copy-start | bytes 9220
  969.1 70.3 %copy-start.68 = (f32[768]{0:T(1024)S(1)}, f32[768]{0:T(1024)}, u32[]{:S(2)}) copy-start(f32[768]{0:T(1024)} %get-tuple-element.57) | copy-start | bytes 9220
  969.1 70.3 %copy-start.69 = (f32[768]{0:T(1024)S(1)}, f32[768]{0:T(1024)}, u32[]{:S(2)}) copy-start(f32[768]{0:T(1024)} %get-tuple-element.68) | copy-start | bytes 9220
  (69 other events, 285.0 us)
Sparse Core Ops, SparseCore 0:
  13.8 47.6 all-gather.4
  297.5 43.3 reduce-scatter.4
  346.8 44.9 all-gather.6
  393.3 44.9 all-gather.8
  464.9 43.3 reduce-scatter.8
  510.9 43.3 reduce-scatter.6
  563.0 44.9 all-gather.10
  938.2 43.3 reduce-scatter.10
  988.6 252.8 all-reduce.4
where the time goes:
time: 1260 us
  waiting for transfers between devices  664 us (53%)
  matrix products  269 us (21%)
  other arithmetic  145 us (12%)
  blocking collectives  104 us (8%)
  local copies, waits for them, and re-layouts  58.9 us (5%)
  between operations  15.3 us (1%)
    ppermute x4, waiting for transfers between devices, from_partner(): return lax.ppermute(block, axis, route)  217 us
    psum x1, waiting for transfers between devices, per_device(): lax.psum((grad_query_weight, grad_query_bias, grad_key_weight, grad_value...  158 us
    psum x1, blocking collectives, per_device(): lax.psum((grad_query_weight, grad_query_bias, grad_key_weight, grad_value...  64 us
    dot_general x4, matrix products, per_device(): jnp.einsum('bqhe,bkhe->bhqk', grad_heads, value_heads, preferred_element_...  56 us
    all_gather x1, waiting for transfers between devices, per_device(): lax.all_gather(first_norm.astype(jnp.bfloat16), 'tp', axis=0, tiled=True)  47.7 us
    all_gather x1, waiting for transfers between devices, per_device(): lax.all_gather(middle_grad.astype(jnp.bfloat16), 'tp', axis=0, tiled=True)  45 us
    all_gather x1, waiting for transfers between devices, per_device(): lax.all_gather(second_norm.astype(jnp.bfloat16), 'tp', axis=0, tiled=True)  44.5 us
    reduce_scatter x1, waiting for transfers between devices, per_device(): lax.psum_scatter(product(attended_rows, out_weight).astype(jnp.bfloat16),...  43.4 us
  transfers between devices with their start and end apart: 13, of which 11 were waited for; matrix products, arithmetic and copies ran while one was open for 11% of the time, Pallas kernels for 0%

commit v1 on v0

--- a/solution.py
+++ b/solution.py
@@ -9,6 +9,23 @@
 SEQ_LEN = 1024
 BLOCK = 256
 EPSILON = 1e-05
+
+
+def laid_out(blocks, dim):
+    shape = list(blocks.shape[1:])
+    shape[dim] *= blocks.shape[0]
+    return jnp.moveaxis(blocks, 0, dim).reshape(shape)
+
+
+def collected_by_bits(shard, axis):
+    size, index = (lax.axis_size(axis), lax.axis_index(axis))
+    tiles, apart = (shard[None], 1)
+    while apart < size:
+        received = lax.ppermute(tiles, axis, [(i, i ^ apart) for i in range(size)])
+        low = index & apart == 0
+        tiles = jnp.concatenate([jnp.where(low, tiles, received), jnp.where(low, received, tiles)])
+        apart *= 2
+    return tiles
 
 
 def from_partner(block, axis, apart):
@@ -197,7 +214,7 @@
     layer_out = (middle + feed_out + down_bias).astype(jnp.bfloat16)
     grad_output = out_grad.astype(jnp.float32)
     grad_down_bias = jnp.sum(grad_output, axis=0)
-    grad_rows_all = lax.all_gather(out_grad, "tp", axis=0, tiled=True)
+    grad_rows_all = laid_out(collected_by_bits(out_grad, "tp"), 0)
     grad_down_weight = product_lt(activated_low, grad_rows_all)
     grad_hidden = gelu_back(product_rt(grad_rows_all, down_weight))[0]
     grad_up_bias = jnp.sum(grad_hidden, axis=0)

time: 1260 us -> 1250 us (level)
    ppermute x0 -> x1, waiting for transfers between devices: none -> 62.5 us  [collected_by_bits(): received = lax.ppermute(tiles, axis, [(i, i ^ apart) for i in range(size)])]
    all_gather x1, waiting for transfers between devices: 44.5 us -> 3.47 us  [per_device(): lax.all_gather(second_norm.astype(jnp.bfloat16), 'tp', axis=0, tiled=True)]
    all_gather x1 -> x0, waiting for transfers between devices: 33.1 us -> none  [per_device(): grad_rows_all = lax.all_gather(out_grad, 'tp', axis=0, tiled=True)]
    unnamed x226 -> x230, local copies, waits for them, and re-layouts: 35.7 us -> 35.8 us
where the time goes in v1:
time: 1250 us
  waiting for transfers between devices  652 us (52%)
  matrix products  267 us (21%)
  other arithmetic  149 us (12%)
  blocking collectives  104 us (8%)
  local copies, waits for them, and re-layouts  59.1 us (5%)
  between operations  15.4 us (1%)
    ppermute x4, waiting for transfers between devices, from_partner(): return lax.ppermute(block, axis, route)  217 us
    psum x1, waiting for transfers between devices, per_device(): lax.psum((grad_query_weight, grad_query_bias, grad_key_weight, grad_value...  157 us
    psum x1, blocking collectives, per_device(): lax.psum((grad_query_weight, grad_query_bias, grad_key_weight, grad_value...  64.2 us
    ppermute x1, waiting for transfers between devices, collected_by_bits(): received = lax.ppermute(tiles, axis, [(i, i ^ apart) for i in range(size)])  62.5 us
    dot_general x4, matrix products, per_device(): jnp.einsum('bqhe,bkhe->bhqk', grad_heads, value_heads, preferred_element_...  56.1 us
    all_gather x1, waiting for transfers between devices, per_device(): lax.all_gather(first_norm.astype(jnp.bfloat16), 'tp', axis=0, tiled=True)  47.7 us
    all_gather x1, waiting for transfers between devices, per_device(): lax.all_gather(middle_grad.astype(jnp.bfloat16), 'tp', axis=0, tiled=True)  45 us
    reduce_scatter x1, waiting for transfers between devices, per_device(): lax.psum_scatter(product(attended_rows, out_weight).astype(jnp.bfloat16),...  43.4 us
  transfers between devices with their start and end apart: 13, of which 11 were waited for; matrix products, arithmetic and copies ran while one was open for 11% of the time, Pallas kernels for 0%

profile of v1, /device:TPU:0, one launch (start us, length us, event | category | flops | bytes accessed | tf_op | source)
XLA Modules:
  0.0 1249.4 jit_solution(3745732338274830790)
XLA Ops:
  13.7 47.7 %all-gather.4.cloned.1.call-done = bf16[2048,768]{1,0:T(8,128)(2,1)} async-done(((bf16[1024,768]{1,0:T(8,128)(2,1)}), bf16[2048,768]{1,0:T(8,128)(2,1)}) %all-gather.4.cloned.1.call-update) | async-done | bytes 3145744 | tf_op jit(solution)/shard_map/all_gather | solution.py:143
  69.7 5.7 collective-permute-done
  81.2 4.5 compare_and_fusion.2
  96.5 6.0 fusion.6
  103.8 6.0 fusion.7
  109.7 107.2 %collective-permute-done.1 = bf16[2,2,2048,384]{2,3,1,0:T(8,128)(2,1)} collective-permute-done((bf16[2,2,2048,384]{2,3,1,0:T(8,128)(2,1)}, bf16[2,2,2048,384]{2,3,1,0:T(8,128)(2,1)}, u32[]{:S(2)}, u32[]{:S(2)}) %collective-permute-start.1) | collective-permute-done | bytes 6291488 | tf_op jit(solution)/shard_map/ppermute | solution.py:38
  224.0 6.2 fusion.8
  233.2 20.6 %exponential_reduce_fusion.2 = (f32[8,6,256]{2,1,0:T(8,128)S(1)}, f32[8,6,256]{2,1,0:T(8,128)S(1)}, f32[8,6,256]{2,1,0:T(8,128)S(1)}, f32[8,6,256]{2,1,0:T(8,128)S(1)}) fusion(f32[8,6,256,256]{2,3,1,0:T(8,128)} %get-tuple-element.88, f32[8,6,256]{2,1,0:T(8,128)S(1)} %maximum_maximum_fusion, pred[8,256,256]{1,2,0:T(8,128)(4,1)S(1)} %copy-done.24, ...), kind=kLoop, calls=%fused_computation.24 | loop fusion | flops 50282496 | bytes 52674560 | tf_op jit(solution)/shard_map/reduce_sum | solution.py:177
  253.8 9.3 fusion.51
  263.1 9.3 fusion.55
  272.4 9.2 fusion.59
  281.6 8.2 fusion.45
  297.5 43.4 %reduce-scatter.5.cloned.1.call-done = bf16[1024,768]{1,0:T(8,128)(2,1)} async-done(((bf16[2048,768]{1,0:T(8,128)(2,1)}), bf16[1024,768]{1,0:T(8,128)(2,1)}) %reduce-scatter.5.cloned.1.call-update) | async-done | bytes 1572880 | tf_op jit(solution)/shard_map/reduce_scatter | solution.py:195
  347.2 62.5 %collective-permute-done.2 = bf16[1,1024,768]{2,1,0:T(8,128)(2,1)} collective-permute-done((bf16[1,1024,768]{2,1,0:T(8,128)(2,1)}, bf16[1,1024,768]{2,1,0:T(8,128)(2,1)}, u32[]{:S(2)}, u32[]{:S(2)}) %collective-permute-start.2) | collective-permute-done | bytes 1572896 | tf_op jit(solution)/shard_map/ppermute | solution.py:24
  417.2 13.5 %multiply_convert_fusion.4 = (bf16[2048,1536]{1,0:T(8,128)(2,1)}, f32[2048,1536]{1,0:T(8,128)}) fusion(f32[1536]{0:T(1024)S(1)} %copy-done.82, bf16[2048,768]{1,0:T(8,128)(2,1)} %all-gather.6.cloned.1.call-done, bf16[768,1536]{1,0:T(8,128)(2,1)S(1)} %copy-done), kind=kOutput, calls=%fused_computation.17 | convolution fusion | flops 4863295488 | bytes 24385536 | tf_op jit(solution)/shard_map/dot_general | solution.py:42
  430.7 14.7 %fusion.107 = (f32[1536]{0:T(1024)}, bf16[2048,1536]{1,0:T(8,128)(2,1)S(1)}) fusion(f32[2048,1536]{1,0:T(8,128)} %get-tuple-element.90, f32[1536]{0:T(1024)S(1)} %copy-done.82, bf16[2048,768]{1,0:T(8,128)(2,1)S(1)} %bitcast.251, bf16[1536,768]{1,0:T(8,128)(2,1)S(1)} %copy-done.78), kind=kOutput, calls=%fused_computation.202 | convolution fusion | flops 4901042688 | bytes 24391680 | tf_op jit(solution)/shard_map/dot_general | solution.py:46
  448.1 6.4 convolution_convert_fusion.1
  456.1 9.2 convolution_convert_fusion.2
  465.4 32.6 %reduce-scatter.9.cloned.1.call-done = bf16[1024,768]{1,0:T(8,128)(2,1)} async-done(((bf16[2048,768]{1,0:T(8,128)(2,1)}), bf16[1024,768]{1,0:T(8,128)(2,1)}) %reduce-scatter.9.cloned.1.call-update) | async-done | bytes 1572880 | tf_op jit(solution)/shard_map/reduce_scatter | solution.py:223
  498.0 4.1 fusion.35
  502.1 42.0 %reduce-scatter.7.cloned.1.call-done = bf16[1024,768]{1,0:T(8,128)(2,1)} async-done(((bf16[2048,768]{1,0:T(8,128)(2,1)}), bf16[1024,768]{1,0:T(8,128)(2,1)}) %reduce-scatter.7.cloned.1.call-update) | async-done | bytes 1572880 | tf_op jit(solution)/shard_map/reduce_scatter | solution.py:208
  544.0 5.6 fusion.104
  552.8 45.0 %all-gather.8.cloned.1.call-done = bf16[2048,768]{1,0:T(8,128)(2,1)} async-done(((bf16[1024,768]{1,0:T(8,128)(2,1)}), bf16[2048,768]{1,0:T(8,128)(2,1)}) %all-gather.8.cloned.1.call-update) | async-done | bytes 3145744 | tf_op jit(solution)/shard_map/all_gather | solution.py:233
  605.3 8.9 fusion.41
  614.2 9.0 fusion.42
  623.2 6.4 fusion.49
  629.6 6.4 fusion.46
  636.0 6.8 fusion.57
  642.8 36.5 %multiply_reduce_fusion.2 = (f32[8,6,256]{2,1,0:T(8,128)S(1)}, f32[8,6,256]{2,1,0:T(8,128)S(1)}, f32[8,6,256]{2,1,0:T(8,128)S(1)}, f32[8,6,256]{2,1,0:T(8,128)S(1)}, f32[8,6,256,256]{2,3,1,0:T(8,128)}) fusion(f32[8,6,256,256]{2,3,1,0:T(8,128)} %get-tuple-element.88, f32[8,6,256]{2,1,0:T(8,128)S(1)} %log_add_fusion, pred[8,256,256]{1,2,0:T(8,128)(4,1)S(1)} %copy-done.25, ...), kind=kOutput, calls=%fused_computation.15 | convolution fusion | flops 465518592 | bytes 106151936 | tf_op jit(solution)/shard_map/bqhe,bkhe->bhqk/dot_general | solution.py:241
  679.4 42.5 %multiply_convert_fusion.1 = (bf16[8,6,256,256]{2,3,1,0:T(8,128)(2,1)}, bf16[8,6,256,256]{2,3,1,0:T(8,128)(2,1)}, bf16[8,6,256,256]{2,3,1,0:T(8,128)(2,1)}, bf16[8,6,256,256]{2,3,1,0:T(8,128)(2,1)}) fusion(f32[8,6,256,256]{2,3,1,0:T(8,128)} %fusion.49, f32[8,6,256,256]{2,3,1,0:T(8,128)} %get-tuple-element.84, f32[8,6,256]{2,1,0:T(8,128)S(1)} %add_add_fusion, ...), kind=kLoop, calls=%fused_computation.10 | loop fusion | flops 75497472 | bytes 128024576 | tf_op jit(solution)/shard_map/convert_element_type | solution.py:251
  721.9 5.0 fusion.43
  732.8 6.5 pad_maximum_fusion.1
  740.8 6.6 multiply_bitcast_fusion
  747.5 4.5 convolution_bitcast_fusion
  751.9 6.5 maximum_bitcast_fusion.1
  758.4 6.6 multiply_bitcast_fusion.1
  765.1 4.5 convolution_bitcast_fusion.1
  772.4 104.5 %collective-permute-done.3 = bf16[2,2,8,256,6,64]{3,5,4,2,1,0:T(8,128)(2,1)} collective-permute-done((bf16[2,2,8,256,6,64]{3,5,4,2,1,0:T(8,128)(2,1)}, bf16[2,2,8,256,6,64]{3,5,4,2,1,0:T(8,128)(2,1)}, u32[]{:S(2)}, u32[]{:S(2)}) %collective-permute-start.3) | collective-permute-done | bytes 6291488 | tf_op jit(solution)/shard_map/ppermute | solution.py:38
  876.9 11.5 maximum_add_fusion
  888.4 5.1 slice.79
  899.3 6.0 bitcast_convert_fusion
  908.6 5.7 slice_add_fusion
  928.3 9.9 fusion.112
  938.3 9.7 fusion.37
  963.4 64.2 %all-reduce.1 = (f32[384]{0:T(512)}, f32[192]{0:T(256)}, f32[1536]{0:T(1024)}) all-reduce(f32[384]{0:T(512)S(1)} %reduce_sum.290, f32[192]{0:T(256)S(1)} %get-tuple-element.64, f32[1536]{0:T(1024)S(1)} %copy-done.71), channel_id=1, replica_groups=mesh['seq'=16,'tp'=2] {'seq'}, use_global_device_ids=true, to_apply=%region_35.36 | all-reduce | flops 2112 | bytes 16896 | tf_op jit(solution)/shard_map/psum | solution.py:306
  1030.6 39.5 %all-reduce = (f32[768]{0:T(1024)}, f32[768]{0:T(1024)}, f32[768]{0:T(1024)}, f32[768]{0:T(1024)}, f32[768]{0:T(1024)}, /*index=5*/f32[768]{0:T(1024)}) all-reduce(f32[768]{0:T(1024)S(1)} %get-tuple-element.20, f32[768]{0:T(1024)S(1)} %get-tuple-element.25, f32[768]{0:T(1024)S(1)} %copy-done.69, ...), channel_id=1, replica_groups=mesh['seq'=16,'tp'=2] {'seq','tp'}, use_global_device_ids=true, to_apply=%region_30.31 | all-reduce | flops 4608 | bytes 36864 | tf_op jit(solution)/shard_map/psum | solution.py:327
  1070.2 4.1 fusion.28
  1074.3 157.4 %all-reduce.5.cloned.1.call-done = (f32[768,384]{1,0:T(8,128)}, f32[768,384]{1,0:T(8,128)}, f32[768,192]{0,1:T(8,128)}, f32[384,768]{1,0:T(8,128)}, f32[768,1536]{1,0:T(8,128)}, /*index=5*/f32[1536,768]{1,0:T(8,128)}) async-done(((f32[768,384]{1,0:T(8,128)}, f32[768,384]{1,0:T(8,128)}, f32[768,192]{0,1:T(8,128)}, f32[384,768]{1,0:T(8,128)}, f32[768,1536]{1,0:T(8,128)}, /*index=5*/f32[1536,768]{1,0:T(8,128)}), ...) | async-done | bytes 13565968 | tf_op jit(solution)/shard_map/psum | solution.py:306
  (326 shorter events, 140.8 us)
Async XLA Ops:
  7.2 410.0 %copy-start = (bf16[768,1536]{1,0:T(8,128)(2,1)S(1)}, bf16[768,1536]{1,0:T(8,128)(2,1)}, u32[]{:S(2)}) copy-start(bf16[768,1536]{1,0:T(8,128)(2,1)} %param.35) | copy-start | bytes 7077892
  7.2 54.2 %all-gather.4.cloned.1.call-start = ((), (), s32[]{:S(2)}) async-start(), calls=%async_computation.4 | async-start | bytes 4718592 | tf_op jit(solution)/shard_map/all_gather | solution.py:143
  9.1 52.3 %copy-start.56 = (bf16[768,192]{0,1:T(8,128)(2,1)S(1)}, bf16[768,192]{0,1:T(8,128)(2,1)}, u32[]{:S(2)}) copy-start(bf16[768,192]{0,1:T(8,128)(2,1)} %param.29) | copy-start | bytes 884740
  9.2 52.3 %copy-start.84 = (f32[192]{0:T(256)S(1)}, f32[192]{0:T(256)}, u32[]{:S(2)}) copy-start(f32[192]{0:T(256)} %param.30) | copy-start | bytes 2308
  13.7 50.9 %copy-start.51 = (bf16[2048,192]{0,1:T(8,128)(2,1)S(1)}, bf16[2048,192]{0,1:T(8,128)(2,1)}, u32[]{:S(2)}) copy-start(bf16[2048,192]{0,1:T(8,128)(2,1)} %param.21) | copy-start | bytes 2359300
  13.7 327.3 %reduce-scatter.5.cloned.1.call-start = ((), (), s32[]{:S(2)}) async-start(), calls=%async_computation.5 | async-start | bytes 4718592 | tf_op jit(solution)/shard_map/reduce_scatter | solution.py:195
  69.7 5.7 collective-permute-start
  79.1 137.9 %collective-permute-start.1 = (bf16[2,2,2048,384]{2,3,1,0:T(8,128)(2,1)}, bf16[2,2,2048,384]{2,3,1,0:T(8,128)(2,1)}, u32[]{:S(2)}, u32[]{:S(2)}) collective-permute-start(bf16[2,2,2048,384]{2,3,1,0:T(8,128)(2,1)} %pad_maximum_fusion), channel_id=1, source_target_pairs={{0,4},{4,0},{2,6},{6,2},{8,12},{12,8},{10,14},{14,10},{16,20},{20,... | collective-permute-start | bytes 18874376 | tf_op jit(solution)/shard_map/ppermute | solution.py:38
  96.0 134.2 %copy-start.8 = (bf16[48,8,8,256]{3,2,1,0:T(8,128)(2,1)}, bf16[48,8,8,256]{3,2,1,0:T(8,128)(2,1)S(1)}, u32[]{:S(2)}) copy-start(bf16[48,8,8,256]{3,2,1,0:T(8,128)(2,1)S(1)} %copy.217) | copy-start | bytes 4718596
  96.5 175.9 %copy-start.20 = (bf16[48,8,8,256]{3,2,1,0:T(8,128)(2,1)}, bf16[48,8,8,256]{3,2,1,0:T(8,128)(2,1)S(1)}, u32[]{:S(2)}) copy-start(bf16[48,8,8,256]{3,2,1,0:T(8,128)(2,1)S(1)} %copy.216) | copy-start | bytes 4718596
  103.2 159.9 %copy-start.28 = (bf16[48,8,8,256]{3,2,1,0:T(8,128)(2,1)}, bf16[48,8,8,256]{3,2,1,0:T(8,128)(2,1)S(1)}, u32[]{:S(2)}) copy-start(bf16[48,8,8,256]{3,2,1,0:T(8,128)(2,1)S(1)} %copy.222) | copy-start | bytes 4718596
  222.6 31.3 %copy-start.22 = (bf16[48,8,8,256]{3,2,1,0:T(8,128)(2,1)}, bf16[48,8,8,256]{3,2,1,0:T(8,128)(2,1)S(1)}, u32[]{:S(2)}) copy-start(bf16[48,8,8,256]{3,2,1,0:T(8,128)(2,1)S(1)} %copy.223) | copy-start | bytes 4718596
  233.2 48.5 %copy-start.2 = (f32[8,6,256,256]{2,3,1,0:T(8,128)}, f32[8,6,256,256]{2,3,1,0:T(8,128)S(1)}, u32[]{:S(2)}) copy-start(f32[8,6,256,256]{2,3,1,0:T(8,128)S(1)} %get-tuple-element.82) | copy-start | bytes 37748740
  297.4 43.5 %copy-start.60 = (f32[768]{0:T(1024)S(1)}, f32[768]{0:T(1024)}, u32[]{:S(2)}) copy-start(f32[768]{0:T(1024)} %param.32) | copy-start | bytes 9220
  297.5 47.2 %copy-start.66 = (f32[768]{0:T(1024)S(1)}, f32[768]{0:T(1024)}, u32[]{:S(2)}) copy-start(f32[768]{0:T(1024)} %param.33) | copy-start | bytes 9220
  297.5 47.2 %copy-start.74 = (f32[768]{0:T(1024)S(1)}, f32[768]{0:T(1024)}, u32[]{:S(2)}) copy-start(f32[768]{0:T(1024)} %param.34) | copy-start | bytes 9220
  297.5 119.7 %all-gather.6.cloned.1.call-start = ((), (), s32[]{:S(2)}) async-start(), calls=%async_computation.6 | async-start | bytes 4718592 | tf_op jit(solution)/shard_map/all_gather | solution.py:204
  346.8 151.2 %reduce-scatter.9.cloned.1.call-start = ((), (), s32[]{:S(2)}) async-start(), calls=%async_computation.8 | async-start | bytes 4718592 | tf_op jit(solution)/shard_map/reduce_scatter | solution.py:223
  346.8 62.9 %collective-permute-start.2 = (bf16[1,1024,768]{2,1,0:T(8,128)(2,1)}, bf16[1,1024,768]{2,1,0:T(8,128)(2,1)}, u32[]{:S(2)}, u32[]{:S(2)}) collective-permute-start(bf16[1,1024,768]{2,1,0:T(8,128)(2,1)} %bitcast.247), channel_id=1, source_target_pairs={{0,1},{1,0},{2,3},{3,2},{4,5},{5,4},{6,7},{7,6},{8,9},{9,8},{10,11... | collective-permute-start | bytes 4718600 | tf_op jit(solution)/shard_map/ppermute | solution.py:24
  417.2 13.6 %copy-start.41 = (bf16[2,1024,768]{2,1,0:T(8,128)(2,1)S(1)}, bf16[2,1024,768]{2,1,0:T(8,128)(2,1)}, u32[]{:S(2)}) copy-start(bf16[2,1024,768]{2,1,0:T(8,128)(2,1)} %pad_maximum_fusion.2) | copy-start | bytes 9437188
  417.2 13.6 %copy-start.78 = (bf16[1536,768]{1,0:T(8,128)(2,1)S(1)}, bf16[1536,768]{1,0:T(8,128)(2,1)}, u32[]{:S(2)}) copy-start(bf16[1536,768]{1,0:T(8,128)(2,1)} %param.37) | copy-start | bytes 7077892
  454.5 89.5 %reduce-scatter.7.cloned.1.call-start = ((), (), s32[]{:S(2)}) async-start(), calls=%async_computation.7 | async-start | bytes 4718592 | tf_op jit(solution)/shard_map/reduce_scatter | solution.py:208
  465.3 32.7 %copy-start.5 = (bf16[1024,768]{1,0:T(8,128)(2,1)S(1)}, bf16[1024,768]{1,0:T(8,128)(2,1)}, u32[]{:S(2)}) copy-start(bf16[1024,768]{1,0:T(8,128)(2,1)} %param.20) | copy-start | bytes 4718596
  465.3 78.7 %copy-start.73 = (f32[768]{0:T(1024)S(1)}, f32[768]{0:T(1024)}, u32[]{:S(2)}) copy-start(f32[768]{0:T(1024)} %param.38) | copy-start | bytes 9220
  465.4 132.5 %all-gather.8.cloned.1.call-start = ((), (), s32[]{:S(2)}) async-start(), calls=%async_computation.9 | async-start | bytes 4718592 | tf_op jit(solution)/shard_map/all_gather | solution.py:233
  551.4 46.4 %copy-start.81 = (bf16[384,768]{1,0:T(8,128)(2,1)S(1)}, bf16[384,768]{1,0:T(8,128)(2,1)}, u32[]{:S(2)}) copy-start(bf16[384,768]{1,0:T(8,128)(2,1)} %param.31) | copy-start | bytes 1769476
  552.7 474.8 %reduce-scatter.11.cloned.1.call-start = ((), (), s32[]{:S(2)}) async-start(), calls=%async_computation.10 | async-start | bytes 4718592 | tf_op jit(solution)/shard_map/reduce_scatter | solution.py:290
  679.4 42.5 %copy-start.9 = (bf16[48,8,8,256]{3,2,1,0:T(8,128)(2,1)S(1)}, bf16[48,8,8,256]{3,2,1,0:T(8,128)(2,1)}, u32[]{:S(2)}) copy-start(bf16[48,8,8,256]{3,2,1,0:T(8,128)(2,1)} %copy-done.8) | copy-start | bytes 4718596
  732.8 14.6 %slice-start.3 = ((s8[12582912]{0:T(1024)(128)(4,1)}), s8[4194304]{0:T(1024)(128)(4,1)S(1)}, s32[]{:S(2)}) async-start(s8[12582912]{0:T(1024)(128)(4,1)} %bitcast.181), calls=%async_computation.15 | async-start | bytes 8388608
  732.8 14.6 %slice-start.4 = ((s8[12582912]{0:T(1024)(128)(4,1)}), s8[4194304]{0:T(1024)(128)(4,1)S(1)}, s32[]{:S(2)}) async-start(s8[12582912]{0:T(1024)(128)(4,1)} %bitcast.181), calls=%async_computation.16 | async-start | bytes 8388608
  739.3 137.6 %collective-permute-start.3 = (bf16[2,2,8,256,6,64]{3,5,4,2,1,0:T(8,128)(2,1)}, bf16[2,2,8,256,6,64]{3,5,4,2,1,0:T(8,128)(2,1)}, u32[]{:S(2)}, u32[]{:S(2)}) collective-permute-start(bf16[2,2,8,256,6,64]{3,5,4,2,1,0:T(8,128)(2,1)} %pad_maximum_fusion.1), channel_id=1, source_target_pairs={{0,4},{4,0},{2,6},{6,2},{8,12},{12,8},{10,14},{14,10},{16,20},{20,... | collective-permute-start | bytes 18874376 | tf_op jit(solution)/shard_map/ppermute | solution.py:38
  751.9 13.1 %slice-start = ((s8[12582912]{0:T(1024)(128)(4,1)}), s8[4194304]{0:T(1024)(128)(4,1)S(1)}, s32[]{:S(2)}) async-start(s8[12582912]{0:T(1024)(128)(4,1)} %bitcast.179), calls=%async_computation.12 | async-start | bytes 8388608
  751.9 13.1 %slice-start.1 = ((s8[12582912]{0:T(1024)(128)(4,1)}), s8[4194304]{0:T(1024)(128)(4,1)S(1)}, s32[]{:S(2)}) async-start(s8[12582912]{0:T(1024)(128)(4,1)} %bitcast.179), calls=%async_computation.13 | async-start | bytes 8388608
  769.5 124.0 %slice-start.8 = ((s8[6291456]{0:T(1024)(128)(4,1)}), s8[4194304]{0:T(1024)(128)(4,1)S(1)}, s32[]{:S(2)}) async-start(s8[6291456]{0:T(1024)(128)(4,1)} %bitcast.193), calls=%async_computation.20 | async-start | bytes 8388608
  769.5 125.1 %slice-start.12 = ((s8[6291456]{0:T(1024)(128)(4,1)}), s8[4194304]{0:T(1024)(128)(4,1)S(1)}, s32[]{:S(2)}) async-start(s8[6291456]{0:T(1024)(128)(4,1)} %bitcast.197), calls=%async_computation.24 | async-start | bytes 8388608
  772.4 121.1 %slice-start.9 = ((s8[6291456]{0:T(1024)(128)(4,1)}), s8[2097152]{0:T(1024)(128)(4,1)S(1)}, s32[]{:S(2)}) async-start(s8[6291456]{0:T(1024)(128)(4,1)} %bitcast.193), calls=%async_computation.21 | async-start | bytes 4194304
  772.4 122.2 %slice-start.13 = ((s8[6291456]{0:T(1024)(128)(4,1)}), s8[2097152]{0:T(1024)(128)(4,1)S(1)}, s32[]{:S(2)}) async-start(s8[6291456]{0:T(1024)(128)(4,1)} %bitcast.197), calls=%async_computation.25 | async-start | bytes 4194304
  893.5 15.1 %collective-permute-start.4 = (bf16[1,2,8,256,6,64]{3,5,4,2,1,0:T(8,128)(2,1)}, bf16[1,2,8,256,6,64]{3,5,4,2,1,0:T(8,128)(2,1)}, u32[]{:S(2)}, u32[]{:S(2)}) collective-permute-start(bf16[1,2,8,256,6,64]{3,5,4,2,1,0:T(8,128)(2,1)} %slice.79), channel_id=1, source_target_pairs={{0,2},{2,0},{4,6},{6,4},{8,10},{10,8},{12,14},{14,12},{16,18},{18,... | collective-permute-start | bytes 9437192 | tf_op jit(solution)/shard_map/ppermute | solution.py:38
  896.5 12.1 slice-start.14
  928.3 303.4 %all-reduce.5.cloned.1.call-start = ((), (), s32[]{:S(2)}) async-start(), calls=%async_computation.11 | async-start | bytes 27131904 | tf_op jit(solution)/shard_map/psum | solution.py:306
  959.9 67.7 %copy-start.6 = (bf16[1024,768]{1,0:T(8,128)(2,1)S(1)}, bf16[1024,768]{1,0:T(8,128)(2,1)}, u32[]{:S(2)}) copy-start(bf16[1024,768]{1,0:T(8,128)(2,1)} %param.20) | copy-start | bytes 4718596
  959.9 67.7 %copy-start.59 = (f32[1024]{0:T(1024)S(1)}, f32[1024]{0:T(1024)}, u32[]{:S(2)}) copy-start(f32[1024]{0:T(1024)} %copy-done.58) | copy-start | bytes 12292
  959.9 67.7 %copy-start.62 = (f32[1024]{0:T(1024)S(1)}, f32[1024]{0:T(1024)}, u32[]{:S(2)}) copy-start(f32[1024]{0:T(1024)} %copy-done.61) | copy-start | bytes 12292
  959.9 67.7 %copy-start.65 = (f32[768]{0:T(1024)S(1)}, f32[768]{0:T(1024)}, u32[]{:S(2)}) copy-start(f32[768]{0:T(1024)} %param.24) | copy-start | bytes 9220
  960.0 70.6 %copy-start.67 = (f32[768]{0:T(1024)S(1)}, f32[768]{0:T(1024)}, u32[]{:S(2)}) copy-start(f32[768]{0:T(1024)} %get-tuple-element.18) | copy-start | bytes 9220
  960.0 70.6 %copy-start.68 = (f32[768]{0:T(1024)S(1)}, f32[768]{0:T(1024)}, u32[]{:S(2)}) copy-start(f32[768]{0:T(1024)} %get-tuple-element.24) | copy-start | bytes 9220
  960.0 70.6 %copy-start.69 = (f32[768]{0:T(1024)S(1)}, f32[768]{0:T(1024)}, u32[]{:S(2)}) copy-start(f32[768]{0:T(1024)} %get-tuple-element.57) | copy-start | bytes 9220
  960.0 70.6 %copy-start.70 = (f32[768]{0:T(1024)S(1)}, f32[768]{0:T(1024)}, u32[]{:S(2)}) copy-start(f32[768]{0:T(1024)} %get-tuple-element.70) | copy-start | bytes 9220
  (71 other events, 302.8 us)
Sparse Core Ops, SparseCore 0:
  13.8 47.6 all-gather.3
  297.6 43.3 reduce-scatter.4
  346.9 70.2 all-gather.5
  454.6 43.3 reduce-scatter.8
  500.7 43.3 reduce-scatter.6
  552.9 44.9 all-gather.7
  928.4 43.3 reduce-scatter.10
  978.8 252.8 all-reduce.4
